TPU v7x, 256 devices: a whole 4x4x8 slice. The times are simulated.
256 devices in a mesh: section: 2 (over core), chan: 32 (over z, x), feed: 4 (over y).
Axes of the slice: x: 4, y: 4, z: 8, core: 2. Of those that a mesh axis runs over, the one named last changes fastest.
Arguments:
- voltages: bfloat16 [2, 1024, 24, 8192], P(None, 'feed', 'section', 'chan'), may hold values from -4 to 4
- positions: int32 [1024], replicated, may hold values from 0 to 1023, each once
- chan_delays: int32 [16, 8192], replicated, may hold values from 0 to 2
- sub_delays: int32 [256, 32], replicated, may hold values from 0 to 4
- boxcars: int32 [3, 2], replicated, may hold values from 1 to 6, as said below
Outputs:
- boxcar_snr: float32 [1024, 24, 3, 256], P(('chan', 'feed'), 'section')
Inputs may be any that keep to these rules, and one draw needn't show every extreme that they name: `boxcars`: column 0 holds the widths 2 to 4, each once; column 1 holds dilations of 1 or more with (width - 1) * dilation <= 6; the filter of width 2 has dilation 6 and the widest filter dilation 1.
All inputs are finite; a program needn't handle non-finite values.
Results may differ from a plain program's by a relative error of at most 0.0033.
Values may be sent and summed in bfloat16 or wider, within the bound.
A program may use at most 64 MiB of HBM per device.

v0:
```python
import math
import jax
import jax.numpy as jnp
from jax import lax
from jax.sharding import PartitionSpec as P

NF = 1024
C = 8192
NK = 16
ND = 256
NW = 3
D1MAX = 2
D2MAX = 4
BOXMAX = 6
SUBCH = 256
EPSILON = 1e-05


def beam_order(positions):
    chan = jnp.arange(32, dtype=jnp.int32)[None, :, None]
    feed = jnp.arange(4, dtype=jnp.int32)[:, None, None]
    low = jnp.arange(8, dtype=jnp.int32)[None, None, :]
    beam_ids = (chan * 32 + feed * 8 + low).reshape(NF)
    phase_ids = beam_ids[:, None] * positions[None, :] % NF
    angles = phase_ids.astype(jnp.float32) * (2.0 * math.pi / NF)
    cosine = jnp.cos(angles)
    sine = jnp.sin(angles)
    upper = jnp.concatenate([cosine, sine], axis=1)
    lower = jnp.concatenate([-sine, cosine], axis=1)
    return jnp.concatenate([upper, lower], axis=0).astype(jnp.bfloat16)


def two_part_dot(values, zero_one):
    high = values.astype(jnp.bfloat16)
    low = (values - high.astype(jnp.float32)).astype(jnp.bfloat16)
    first = jnp.dot(high, zero_one, preferred_element_type=jnp.float32)
    return first + jnp.dot(low, zero_one, preferred_element_type=jnp.float32)


def channel_selector(delays, span_t):
    local = delays.shape[1]
    times = jnp.arange(span_t, dtype=jnp.int32)[:, None, None, None]
    outs = jnp.arange(span_t + D1MAX, dtype=jnp.int32)[None, None, :, None]
    chosen = times + D1MAX - outs == jnp.transpose(delays)[None, :, None, :]
    return chosen.astype(jnp.bfloat16).reshape(span_t * local, (span_t + D1MAX) * NK)


def subband_selector(sub_delays):
    offsets = jnp.arange(D2MAX + 1, dtype=jnp.int32)[:, None, None, None]
    matches = jnp.transpose(sub_delays)[None, :, None, :] == offsets
    trial_k = jnp.arange(ND, dtype=jnp.int32) * NK // ND
    own = jnp.arange(NK, dtype=jnp.int32)[:, None] == trial_k[None, :]
    weights = matches & own[None, None, :, :]
    return weights.astype(jnp.bfloat16).reshape(D2MAX + 1, -1, ND)


def boxcar_filter(extended, boxcars, span_t):
    outputs = []
    for filter_index in range(NW):
        width_now = boxcars[filter_index, 0]
        stride_now = boxcars[filter_index, 1]
        summed = extended[:, :span_t]
        for offset in range(1, NW + 1):
            start = jnp.minimum(offset * stride_now, BOXMAX)
            window_part = lax.dynamic_slice_in_dim(extended, start, span_t, 1)
            summed = summed + jnp.where(offset < width_now, window_part, 0.0)
        outputs.append(summed * lax.rsqrt(width_now.astype(jnp.float32)))
    return jnp.stack(outputs, axis=2)


def per_device(voltages, positions, chan_delays, sub_delays, boxcars):
    gathered = lax.all_to_all(voltages, "feed", split_axis=3, concat_axis=1, tiled=True)
    span_t = gathered.shape[2]
    local = gathered.shape[3]
    table = beam_order(positions)
    flat = gathered.reshape(2 * NF, span_t * local)
    product = jnp.dot(table, flat, preferred_element_type=jnp.float32)
    real_part = product[:NF]
    imag_part = product[NF:]
    power = (real_part * real_part + imag_part * imag_part).reshape(NF, span_t, local)
    section_count = lax.axis_size("section")
    totals = lax.psum(jnp.sum(power, axis=1), "section")
    level = totals / (span_t * section_count)
    normed = power / (level[:, None, :] + EPSILON) - 1.0
    start = lax.axis_index("chan") * SUBCH + lax.axis_index("feed") * local
    delays = lax.dynamic_slice_in_dim(chan_delays, start, local, 1)
    partial = two_part_dot(normed.reshape(NF, span_t * local), channel_selector(delays, span_t))
    summed = lax.psum_scatter(partial, "feed", scatter_dimension=0, tiled=True)
    span_u = span_t + D1MAX
    blocks = summed.reshape(lax.axis_size("chan"), -1, span_u * NK)
    turned = lax.all_to_all(blocks, "chan", split_axis=0, concat_axis=0, tiled=True)
    bands, beams = (turned.shape[0], turned.shape[1])
    subband = jnp.transpose(turned.reshape(bands, beams, span_u, NK), (1, 2, 0, 3))
    padded = jnp.pad(subband.reshape(beams, span_u, bands * NK), ((0, 0), (D2MAX, D2MAX), (0, 0)))
    span_v = span_u + D2MAX
    shifted = jnp.concatenate([padded[:, d : d + span_v] for d in range(D2MAX + 1)], axis=2)
    weights = subband_selector(sub_delays).reshape(-1, ND)
    dedispersed = two_part_dot(shifted.reshape(beams * span_v, -1), weights) * (1.0 / math.sqrt(C))
    dedispersed = dedispersed.reshape(beams, span_v, ND)
    later = lax.ppermute(dedispersed[:, :span_t], "section", [(1, 0)])
    extended = jnp.pad(dedispersed[:, BOXMAX:], ((0, 0), (0, BOXMAX), (0, 0)))
    extended = extended + jnp.pad(later, ((0, 0), (BOXMAX, 0), (0, 0)))
    return boxcar_filter(extended, boxcars, span_t)


def solution(mesh):
    return jax.shard_map(
        per_device,
        mesh=mesh,
        in_specs=(P(None, "feed", "section", "chan"), P(), P(), P(), P()),
        out_specs=P(("chan", "feed"), "section", None, None),
        check_vma=False,
    )
```

profile of v0, /device:TPU:1, one launch (start us, length us, event | category | flops | bytes accessed | tf_op | source)
XLA Modules:
  0.0 219.8 jit_solution(1089772544984727857)
XLA Ops:
  6.5 0.0 copy-start
  6.5 8.9 %copy.44 = bf16[2,256,12,256]{1,0,2,3:T(2,128)(2,1)} copy(bf16[2,256,12,256]{3,1,2,0:T(8,128)(2,1)} %param.5) | data formatting | bytes 6291456 | tf_op args[0]
  15.4 0.0 copy-start.5
  15.4 5.1 %all-to-all-start = ((bf16[2,256,12,256]{1,0,2,3:T(2,128)(2,1)}), bf16[2,256,12,256]{1,0,2,3:T(2,128)(2,1)}, u32[]{:S(2)}, u32[]{:S(2)}) async-start(bf16[2,256,12,256]{1,0,2,3:T(2,128)(2,1)} %copy.44), calls=%async_computation | async-start | bytes 6291456 | tf_op jit(solution)/shard_map/all_to_all | solution.py:72
  20.5 0.0 all-reduce.5.cloned.1.call-start
  20.5 0.1 broadcast_add_fusion
  20.6 0.1 iota_add_fusion
  20.7 0.1 add.154
  20.8 0.0 copy-done.5
  20.8 19.0 %fusion.14 = (bf16[1024,1024]{1,0:T(8,128)(2,1)S(1)}, bf16[1024,1024]{1,0:T(8,128)(2,1)}, bf16[1024,1024]{1,0:T(8,128)(2,1)}) fusion(s32[1024]{0:T(1024)S(1)} %copy-done.5, s32[1024]{0:T(1024)S(1)} %add.154), kind=kLoop, calls=%fused_computation.25 | loop fusion | flops 18874368 | bytes 6299648 | tf_op jit(solution)/shard_map/convert.5
  39.8 16.4 %all-to-all-done = bf16[2,256,12,256]{1,0,2,3:T(2,128)(2,1)} async-done(((bf16[2,256,12,256]{1,0,2,3:T(2,128)(2,1)}), bf16[2,256,12,256]{1,0,2,3:T(2,128)(2,1)}, u32[]{:S(2)}, u32[]{:S(2)}) %all-to-all-start) | async-done | bytes 3145760 | tf_op jit(solution)/shard_map/all_to_all | solution.py:72
  56.2 2.6 %copy.45 = bf16[2,256,12,256]{1,3,2,0:T(8,128)(2,1)S(1)} copy(bf16[2,256,12,256]{1,0,2,3:T(2,128)(2,1)} %all-to-all-done) | data formatting | bytes 6291456 | tf_op jit(solution)/shard_map/all_to_all | solution.py:72
  58.8 4.1 %copy.46 = bf16[2,4,256,12,64]{2,1,0,4,3:T(4,128)(2,1)} copy(bf16[2,4,256,12,64]{2,4,1,3,0:T(8,128)(2,1)S(1)} %bitcast.56) | data formatting | bytes 6291456 | tf_op jit(solution)/shard_map/all_to_all | solution.py:72
  62.9 6.1 %reshape.237 = bf16[2048,768]{0,1:T(8,128)(2,1)} reshape(bf16[2,4,256,12,64]{2,1,0,4,3:T(4,128)(2,1)} %copy.46) | data formatting | bytes 6291456 | tf_op jit(solution)/shard_map/reshape | solution.py:76
  69.0 16.8 %fusion = f32[2048,768]{0,1:T(8,128)S(1)} fusion(bf16[2048,768]{0,1:T(8,128)(2,1)} %reshape.237, bf16[1024,1024]{1,0:T(8,128)(2,1)} %get-tuple-element.16, bf16[1024,1024]{1,0:T(8,128)(2,1)} %get-tuple-element.15, bf16[1024,1024]{1,0:T(8,128)(2,1)S(1)} %get-tuple-element.14), kind=kOutput, calls=%fused_computation | convolution fusion | flops 6476005376 | bytes 15728640 | tf_op jit(solution)/shard_map/dot_general | solution.py:77
  85.9 0.0 copy-start.1
  85.9 2.8 %fusion.11 = f32[1024,768]{0,1:T(8,128)} fusion(f32[2048,768]{0,1:T(8,128)S(1)} %fusion), kind=kLoop, calls=%fused_computation.19 | loop fusion | flops 2359296 | bytes 9437184 | tf_op jit(solution)/shard_map/add | solution.py:80
  88.7 0.8 copy-done.1
  89.6 2.8 %reduce_sum.9 = f32[1024,64]{0,1:T(8,128)} reduce(f32[1024,12,64]{0,2,1:T(8,128)} %bitcast.57, f32[]{:T(128)} %constant.80.clone.1), dimensions={1}, to_apply=%region_0.1 | reduce | flops 720896 | bytes 3407876 | tf_op jit(solution)/shard_map/reduce_sum | solution.py:82
  92.4 0.0 all-reduce.5.cloned.1.call-update
  92.4 0.2 reduce-scatter.2.cloned.1.call-start
  92.6 0.0 copy-done
  92.6 0.1 dynamic-slice_bitcast_fusion
  92.7 0.3 broadcast_compare_fusion
  93.0 0.7 eq.57
  93.8 32.2 %all-reduce.5.cloned.1.call-done = f32[1024,64]{0,1:T(8,128)} async-done(((f32[1024,64]{0,1:T(8,128)}), f32[1024,64]{0,1:T(8,128)}) %all-reduce.5.cloned.1.call-update) | async-done | bytes 262160 | tf_op jit(solution)/shard_map/psum | solution.py:82
  126.0 1.0 multiply_add_fusion
  126.9 3.6 %fusion.12 = f32[1024,768]{0,1:T(8,128)S(1)} fusion(f32[1024,64]{0,1:T(8,128)S(1)} %multiply_add_fusion, f32[2048,768]{0,1:T(8,128)} %copy-done.1), kind=kLoop, calls=%fused_computation.22 | loop fusion | flops 3932160 | bytes 9699328 | tf_op jit(solution)/shard_map/sub | solution.py:84
  130.6 0.5 fusion.19
  131.1 0.0 copy-start.3
  131.1 1.5 fusion.16
  132.6 0.0 reduce-scatter.2.cloned.1.call-update
  132.6 0.0 copy-done.3
  132.7 25.1 %reduce-scatter.2.cloned.1.call-done = f32[256,224]{0,1:T(8,128)} async-done(((f32[1024,224]{0,1:T(8,128)}), f32[256,224]{0,1:T(8,128)}) %reduce-scatter.2.cloned.1.call-update) | async-done | bytes 229392 | tf_op jit(solution)/shard_map/reduce_scatter | solution.py:88
  157.8 1.8 copy.47
  159.6 9.6 %all-to-all-start.1 = ((f32[32,8,224]{2,1,0:T(8,128)}), f32[32,8,224]{2,1,0:T(8,128)S(1)}, u32[]{:S(2)}, u32[]{:S(2)}) async-start(f32[32,8,224]{2,1,0:T(8,128)} %bitcast.5), calls=%async_computation.2 | async-start | bytes 524288 | tf_op jit(solution)/shard_map/all_to_all | solution.py:91
  169.2 1.2 broadcast_and_fusion
  170.4 9.2 %all-to-all-done.1 = f32[32,8,224]{2,1,0:T(8,128)S(1)} async-done(((f32[32,8,224]{2,1,0:T(8,128)}), f32[32,8,224]{2,1,0:T(8,128)S(1)}, u32[]{:S(2)}, u32[]{:S(2)}) %all-to-all-start.1) | async-done | bytes 229408 | tf_op jit(solution)/shard_map/all_to_all | solution.py:91
  179.6 0.3 copy.48
  179.9 0.6 copy.49
  180.5 1.3 reshape.241
  181.8 0.2 pad_slice_fusion
  181.9 0.2 copy.50
  182.2 0.8 constant_dynamic-update-slice_fusion.4
  183.0 0.2 copy.51
  183.2 0.0 copy-start.2
  183.2 0.2 copy.52
  183.4 0.2 copy.53
  183.7 0.2 copy.54
  183.9 0.7 constant_dynamic-update-slice_fusion.3
  184.6 0.8 constant_dynamic-update-slice_fusion.2
  185.4 0.8 constant_dynamic-update-slice_fusion.1
  186.1 0.7 constant_dynamic-update-slice_fusion
  186.9 0.0 copy-done.2
  186.9 0.0 copy-start.4
  186.9 1.9 fusion.22
  188.8 2.4 %fusion.17 = f32[144,256]{1,0:T(8,128)S(1)} fusion(f32[144,256]{1,0:T(8,128)S(1)} %fusion.22, pred[2560,256]{1,0:T(8,128)(4,1)S(1)} %bitcast.60, f32[144,2560]{1,0:T(8,128)} %constant_dynamic-update-slice_fusion), kind=kOutput, calls=%fused_computation.31 | convolution fusion | flops 190291968 | bytes 2424832 | tf_op jit(solution)/shard_map/dot_general | solution.py:37
  191.2 5.7 %collective-permute-start = (f32[8,12,256]{2,1,0:T(8,128)S(1)}, f32[8,12,256]{2,1,0:T(8,128)S(1)}, u32[]{:S(2)}, u32[]{:S(2)}) collective-permute-start(f32[8,12,256]{2,1,0:T(8,128)S(1)} %get-tuple-element.12), channel_id=1, source_target_pairs={{128,0},{129,1},{130,2},{131,3},{132,4},{133,5},{134,6},{135,7},{1... | collective-permute-start | bytes 294920 | tf_op jit(solution)/shard_map/ppermute | solution.py:100
  196.9 0.0 copy-done.4
  196.9 0.7 fusion.60
  211.0 0.0 collective-permute-done
  211.1 0.3 fusion.28
  211.3 0.7 fusion.36
  212.1 0.9 copy.55
  (15 shorter events, 0.3 us)
Async XLA Ops:
  6.5 86.1 %copy-start = (s32[16,8192]{1,0:T(8,128)S(1)}, s32[16,8192]{1,0:T(8,128)}, u32[]{:S(2)}) copy-start(s32[16,8192]{1,0:T(8,128)} %param.7) | copy-start | bytes 1572868
  15.4 5.4 %copy-start.5 = (s32[1024]{0:T(1024)S(1)}, s32[1024]{0:T(1024)}, u32[]{:S(2)}) copy-start(s32[1024]{0:T(1024)} %param.6) | copy-start | bytes 12292
  15.4 40.8 %all-to-all-start = ((bf16[2,256,12,256]{1,0,2,3:T(2,128)(2,1)}), bf16[2,256,12,256]{1,0,2,3:T(2,128)(2,1)}, u32[]{:S(2)}, u32[]{:S(2)}) async-start(bf16[2,256,12,256]{1,0,2,3:T(2,128)(2,1)} %copy.44), calls=%async_computation | async-start | bytes 6291456 | tf_op jit(solution)/shard_map/all_to_all | solution.py:72
  20.5 105.4 %all-reduce.5.cloned.1.call-start = ((), (), s32[]{:S(2)}) async-start(), calls=%async_computation.3 | async-start | bytes 524288 | tf_op jit(solution)/shard_map/psum | solution.py:82
  85.9 3.7 %copy-start.1 = (f32[2048,768]{0,1:T(8,128)}, f32[2048,768]{0,1:T(8,128)S(1)}, u32[]{:S(2)}) copy-start(f32[2048,768]{0,1:T(8,128)S(1)} %fusion) | copy-start | bytes 18874372
  92.4 65.4 %reduce-scatter.2.cloned.1.call-start = ((), (), s32[]{:S(2)}) async-start(), calls=%async_computation.4 | async-start | bytes 1146880 | tf_op jit(solution)/shard_map/reduce_scatter | solution.py:88
  131.1 1.5 copy-start.3
  159.6 20.0 %all-to-all-start.1 = ((f32[32,8,224]{2,1,0:T(8,128)}), f32[32,8,224]{2,1,0:T(8,128)S(1)}, u32[]{:S(2)}, u32[]{:S(2)}) async-start(f32[32,8,224]{2,1,0:T(8,128)} %bitcast.5), calls=%async_computation.2 | async-start | bytes 524288 | tf_op jit(solution)/shard_map/all_to_all | solution.py:91
  183.2 3.7 %copy-start.2 = (pred[5,32,16,256]{3,2,1,0:T(8,128)(4,1)S(1)}, pred[5,32,16,256]{3,2,1,0:T(8,128)(4,1)}, u32[]{:S(2)}) copy-start(pred[5,32,16,256]{3,2,1,0:T(8,128)(4,1)} %broadcast_and_fusion) | copy-start | bytes 1966084
  186.9 10.0 %copy-start.4 = (s32[3,2]{0,1:T(2,128)S(1)}, s32[3,2]{0,1:T(2,128)}, u32[]{:S(2)}) copy-start(s32[3,2]{0,1:T(2,128)} %param.9) | copy-start | bytes 76
  191.2 19.8 %collective-permute-start = (f32[8,12,256]{2,1,0:T(8,128)S(1)}, f32[8,12,256]{2,1,0:T(8,128)S(1)}, u32[]{:S(2)}, u32[]{:S(2)}) collective-permute-start(f32[8,12,256]{2,1,0:T(8,128)S(1)} %get-tuple-element.12), channel_id=1, source_target_pairs={{128,0},{129,1},{130,2},{131,3},{132,4},{133,5},{134,6},{135,7},{1... | collective-permute-start | bytes 294920 | tf_op jit(solution)/shard_map/ppermute | solution.py:100
Sparse Core Ops, SparseCore 0:
  92.5 33.3 all-reduce.4
  132.7 25.0 reduce-scatter.1
where the time goes:
time: 221 us; the launch traced here: 220 us
  waiting for transfers between devices  82.9 us (38%)
  local copies, waits for them, and re-layouts  34 us (15%)
  other arithmetic  32.1 us (15%)
  between operations  27.2 us (12%)
  matrix products  23.1 us (10%)
  starting transfers between devices  20.6 us (9%)
    psum x1, waiting for transfers between devices, per_device(): totals = lax.psum(jnp.sum(power, axis=1), 'section')  32.2 us
    reduce_scatter x1, waiting for transfers between devices, per_device(): summed = lax.psum_scatter(partial, 'feed', scatter_dimension=0, tiled=True)  25.1 us
    another operation x1, other arithmetic  19 us
    dot_general x1, matrix products, per_device(): product = jnp.dot(table, flat, preferred_element_type=jnp.float32)  16.8 us
    all_to_all x1, waiting for transfers between devices, per_device(): lax.all_to_all(voltages, 'feed', split_axis=3, concat_axis=1, tiled=True)  16.4 us
    unnamed x17, local copies, waits for them, and re-layouts  12.7 us
    all_to_all x1, starting transfers between devices, per_device(): lax.all_to_all(blocks, 'chan', split_axis=0, concat_axis=0, tiled=True)  9.56 us
    all_to_all x1, waiting for transfers between devices, per_device(): lax.all_to_all(blocks, 'chan', split_axis=0, concat_axis=0, tiled=True)  9.17 us
  transfers between devices with their start and end apart: 5, of which 4 were waited for; matrix products, arithmetic and copies ran while one was open for 10% of the time, Pallas kernels for 0%

commit v1 on v0

--- a/solution.py
+++ b/solution.py
@@ -14,6 +14,12 @@
 BOXMAX = 6
 SUBCH = 256
 EPSILON = 1e-05
+
+
+def summed_here(x, axis):
+    shards = lax.all_gather(x, axis, axis=0, tiled=False)
+    acc = shards.sum(axis=0)
+    return acc
 
 
 def beam_order(positions):
@@ -79,7 +85,7 @@
     imag_part = product[NF:]
     power = (real_part * real_part + imag_part * imag_part).reshape(NF, span_t, local)
     section_count = lax.axis_size("section")
-    totals = lax.psum(jnp.sum(power, axis=1), "section")
+    totals = summed_here(jnp.sum(power, axis=1), "section")
     level = totals / (span_t * section_count)
     normed = power / (level[:, None, :] + EPSILON) - 1.0
     start = lax.axis_index("chan") * SUBCH + lax.axis_index("feed") * local

time: 221 us -> 192 us (0.87)
  waiting for transfers between devices: 82.9 us -> 49.6 us
  blocking collectives: 0 us -> 5.28 us
    psum x1 -> x0, waiting for transfers between devices: 32.2 us -> none  [per_device(): totals = lax.psum(jnp.sum(power, axis=1), 'section')]
    all_gather x0 -> x1, blocking collectives: none -> 5.28 us  [summed_here(): shards = lax.all_gather(x, axis, axis=0, tiled=False)]
  transfers between devices with their start and end apart: 5 -> 4, of which waited for: 4 -> 3; matrix products, arithmetic and copies ran while one was open for 10% -> 12% of each run, Pallas kernels for 0% -> 0%
where the time goes in v1:
time: 192 us; the launch traced here: 191 us
  waiting for transfers between devices  49.6 us (26%)
  local copies, waits for them, and re-layouts  34.5 us (18%)
  other arithmetic  31 us (16%)
  between operations  27.1 us (14%)
  matrix products  23.1 us (12%)
  starting transfers between devices  20.4 us (11%)
  blocking collectives  5.28 us (3%)
    reduce_scatter x1, waiting for transfers between devices, per_device(): summed = lax.psum_scatter(partial, 'feed', scatter_dimension=0, tiled=True)  25.2 us
    another operation x1, other arithmetic  19 us
    dot_general x1, matrix products, per_device(): product = jnp.dot(table, flat, preferred_element_type=jnp.float32)  16.8 us
    all_to_all x1, waiting for transfers between devices, per_device(): lax.all_to_all(voltages, 'feed', split_axis=3, concat_axis=1, tiled=True)  15.2 us
    unnamed x17, local copies, waits for them, and re-layouts  12.8 us
    all_to_all x1, starting transfers between devices, per_device(): lax.all_to_all(blocks, 'chan', split_axis=0, concat_axis=0, tiled=True)  9.57 us
    all_to_all x1, waiting for transfers between devices, per_device(): lax.all_to_all(blocks, 'chan', split_axis=0, concat_axis=0, tiled=True)  9.17 us
    all_to_all x2, local copies, waits for them, and re-layouts, per_device(): lax.all_to_all(voltages, 'feed', split_axis=3, concat_axis=1, tiled=True)  6.73 us
  transfers between devices with their start and end apart: 4, of which 3 were waited for; matrix products, arithmetic and copies ran while one was open for 12% of the time, Pallas kernels for 0%

profile of v1, /device:TPU:1, one launch (start us, length us, event | category | flops | bytes accessed | tf_op | source)
XLA Modules:
  0.0 190.9 jit_solution(1609677396335200799)
XLA Ops:
  6.5 0.0 copy-start
  6.5 8.9 %copy.44 = bf16[2,256,12,256]{1,0,2,3:T(2,128)(2,1)} copy(bf16[2,256,12,256]{3,1,2,0:T(8,128)(2,1)} %param.5) | data formatting | bytes 6291456 | tf_op args[0]
  15.4 0.0 copy-start.5
  15.4 5.1 %all-to-all-start = ((bf16[2,256,12,256]{1,0,2,3:T(2,128)(2,1)}), bf16[2,256,12,256]{1,0,2,3:T(2,128)(2,1)}, u32[]{:S(2)}, u32[]{:S(2)}) async-start(bf16[2,256,12,256]{1,0,2,3:T(2,128)(2,1)} %copy.44), calls=%async_computation | async-start | bytes 6291456 | tf_op jit(solution)/shard_map/all_to_all | solution.py:78
  20.5 0.0 reduce-scatter.2.cloned.1.call-start
  20.6 0.1 broadcast_add_fusion
  20.6 0.1 iota_add_fusion
  20.7 0.1 add.156
  20.8 0.0 copy-done
  20.8 0.1 dynamic-slice_bitcast_fusion
  20.9 0.3 broadcast_compare_fusion
  21.3 0.7 eq.57
  22.0 0.0 copy-done.5
  22.0 19.0 %fusion.14 = (bf16[1024,1024]{1,0:T(8,128)(2,1)S(1)}, bf16[1024,1024]{1,0:T(8,128)(2,1)}, bf16[1024,1024]{1,0:T(8,128)(2,1)}) fusion(s32[1024]{0:T(1024)S(1)} %copy-done.5, s32[1024]{0:T(1024)S(1)} %add.156), kind=kLoop, calls=%fused_computation.25 | loop fusion | flops 18874368 | bytes 6299648 | tf_op jit(solution)/shard_map/convert.5
  41.0 15.2 %all-to-all-done = bf16[2,256,12,256]{1,0,2,3:T(2,128)(2,1)} async-done(((bf16[2,256,12,256]{1,0,2,3:T(2,128)(2,1)}), bf16[2,256,12,256]{1,0,2,3:T(2,128)(2,1)}, u32[]{:S(2)}, u32[]{:S(2)}) %all-to-all-start) | async-done | bytes 3145760 | tf_op jit(solution)/shard_map/all_to_all | solution.py:78
  56.2 2.6 %copy.45 = bf16[2,256,12,256]{1,3,2,0:T(8,128)(2,1)S(1)} copy(bf16[2,256,12,256]{1,0,2,3:T(2,128)(2,1)} %all-to-all-done) | data formatting | bytes 6291456 | tf_op jit(solution)/shard_map/all_to_all | solution.py:78
  58.9 4.1 %copy.46 = bf16[2,4,256,12,64]{2,1,0,4,3:T(4,128)(2,1)} copy(bf16[2,4,256,12,64]{2,4,1,3,0:T(8,128)(2,1)S(1)} %bitcast.58) | data formatting | bytes 6291456 | tf_op jit(solution)/shard_map/all_to_all | solution.py:78
  63.0 6.1 %reshape.240 = bf16[2048,768]{0,1:T(8,128)(2,1)} reshape(bf16[2,4,256,12,64]{2,1,0,4,3:T(4,128)(2,1)} %copy.46) | data formatting | bytes 6291456 | tf_op jit(solution)/shard_map/reshape | solution.py:82
  69.1 16.8 %fusion = f32[2048,768]{0,1:T(8,128)S(1)} fusion(bf16[2048,768]{0,1:T(8,128)(2,1)} %reshape.240, bf16[1024,1024]{1,0:T(8,128)(2,1)} %get-tuple-element.16, bf16[1024,1024]{1,0:T(8,128)(2,1)} %get-tuple-element.15, bf16[1024,1024]{1,0:T(8,128)(2,1)S(1)} %get-tuple-element.14), kind=kOutput, calls=%fused_computation | convolution fusion | flops 6476005376 | bytes 15728640 | tf_op jit(solution)/shard_map/dot_general | solution.py:83
  85.9 0.0 copy-start.1
  85.9 2.8 %fusion.11 = f32[1024,768]{0,1:T(8,128)} fusion(f32[2048,768]{0,1:T(8,128)S(1)} %fusion), kind=kLoop, calls=%fused_computation.19 | loop fusion | flops 2359296 | bytes 9437184 | tf_op jit(solution)/shard_map/add | solution.py:86
  88.8 0.8 copy-done.1
  89.6 2.1 %reduce_sum.18 = f32[1024,64]{0,1:T(8,128)S(1)} reduce(f32[1024,12,64]{0,2,1:T(8,128)} %bitcast.59, f32[]{:T(128)} %constant.80.clone.1), dimensions={1}, to_apply=%region_0.1 | reduce | flops 720896 | bytes 3407876 | tf_op jit(solution)/shard_map/reduce_sum | solution.py:88
  91.7 5.3 %all-gather = f32[2048,64]{0,1:T(8,128)S(1)} all-gather(f32[1024,64]{0,1:T(8,128)S(1)} %reduce_sum.18), channel_id=2, replica_groups=mesh['section'=2,'chan'=32,'feed'=4] {'section'}, dimensions={0}, use_global_device_ids=true | all-gather | bytes 786432 | tf_op jit(solution)/shard_map/all_gather | solution.py:20
  97.0 0.4 reshape.246
  97.4 0.6 reduce_sum.19
  98.1 3.6 %fusion.12 = f32[1024,768]{0,1:T(8,128)S(1)} fusion(f32[1024,64]{0,1:T(8,128)S(1)} %multiply_add_fusion, f32[2048,768]{0,1:T(8,128)} %copy-done.1), kind=kLoop, calls=%fused_computation.22 | loop fusion | flops 3932160 | bytes 9699328 | tf_op jit(solution)/shard_map/sub | solution.py:90
  101.8 0.5 fusion.19
  102.3 0.0 copy-start.3
  102.3 1.5 fusion.16
  103.8 0.0 reduce-scatter.2.cloned.1.call-update
  103.8 0.0 copy-done.3
  103.9 25.2 %reduce-scatter.2.cloned.1.call-done = f32[256,224]{0,1:T(8,128)} async-done(((f32[1024,224]{0,1:T(8,128)}), f32[256,224]{0,1:T(8,128)}) %reduce-scatter.2.cloned.1.call-update) | async-done | bytes 229392 | tf_op jit(solution)/shard_map/reduce_scatter | solution.py:94
  129.1 1.8 copy.47
  130.8 9.6 %all-to-all-start.1 = ((f32[32,8,224]{2,1,0:T(8,128)}), f32[32,8,224]{2,1,0:T(8,128)S(1)}, u32[]{:S(2)}, u32[]{:S(2)}) async-start(f32[32,8,224]{2,1,0:T(8,128)} %bitcast.5), calls=%async_computation.2 | async-start | bytes 524288 | tf_op jit(solution)/shard_map/all_to_all | solution.py:97
  140.4 1.2 broadcast_and_fusion
  141.6 9.2 %all-to-all-done.1 = f32[32,8,224]{2,1,0:T(8,128)S(1)} async-done(((f32[32,8,224]{2,1,0:T(8,128)}), f32[32,8,224]{2,1,0:T(8,128)S(1)}, u32[]{:S(2)}, u32[]{:S(2)}) %all-to-all-start.1) | async-done | bytes 229408 | tf_op jit(solution)/shard_map/all_to_all | solution.py:97
  150.8 0.3 copy.48
  151.1 0.6 copy.49
  151.7 1.3 reshape.244
  153.0 0.2 pad_slice_fusion
  153.2 0.2 copy.50
  153.4 0.8 constant_dynamic-update-slice_fusion.4
  154.2 0.2 copy.51
  154.4 0.0 copy-start.2
  154.4 0.2 copy.52
  154.7 0.2 copy.53
  154.9 0.2 copy.54
  155.1 0.8 constant_dynamic-update-slice_fusion.3
  155.9 0.7 constant_dynamic-update-slice_fusion.2
  156.6 0.8 constant_dynamic-update-slice_fusion.1
  157.4 0.7 constant_dynamic-update-slice_fusion
  158.1 0.0 copy-done.2
  158.1 0.0 copy-start.4
  158.1 1.9 fusion.22
  160.0 2.3 %fusion.17 = f32[144,256]{1,0:T(8,128)S(1)} fusion(f32[144,256]{1,0:T(8,128)S(1)} %fusion.22, pred[2560,256]{1,0:T(8,128)(4,1)S(1)} %bitcast.62, f32[144,2560]{1,0:T(8,128)} %constant_dynamic-update-slice_fusion), kind=kOutput, calls=%fused_computation.31 | convolution fusion | flops 190291968 | bytes 2424832 | tf_op jit(solution)/shard_map/dot_general | solution.py:43
  162.4 5.7 %collective-permute-start = (f32[8,12,256]{2,1,0:T(8,128)S(1)}, f32[8,12,256]{2,1,0:T(8,128)S(1)}, u32[]{:S(2)}, u32[]{:S(2)}) collective-permute-start(f32[8,12,256]{2,1,0:T(8,128)S(1)} %get-tuple-element.12), channel_id=1, source_target_pairs={{128,0},{129,1},{130,2},{131,3},{132,4},{133,5},{134,6},{135,7},{1... | collective-permute-start | bytes 294920 | tf_op jit(solution)/shard_map/ppermute | solution.py:106
  168.1 0.0 copy-done.4
  168.1 0.7 fusion.60
  182.2 0.0 collective-permute-done
  182.2 0.3 fusion.28
  182.5 0.7 fusion.36
  183.2 0.9 copy.55
  (16 shorter events, 0.4 us)
Async XLA Ops:
  6.5 14.3 %copy-start = (s32[16,8192]{1,0:T(8,128)S(1)}, s32[16,8192]{1,0:T(8,128)}, u32[]{:S(2)}) copy-start(s32[16,8192]{1,0:T(8,128)} %param.7) | copy-start | bytes 1572868
  15.4 6.6 %copy-start.5 = (s32[1024]{0:T(1024)S(1)}, s32[1024]{0:T(1024)}, u32[]{:S(2)}) copy-start(s32[1024]{0:T(1024)} %param.6) | copy-start | bytes 12292
  15.4 40.8 %all-to-all-start = ((bf16[2,256,12,256]{1,0,2,3:T(2,128)(2,1)}), bf16[2,256,12,256]{1,0,2,3:T(2,128)(2,1)}, u32[]{:S(2)}, u32[]{:S(2)}) async-start(bf16[2,256,12,256]{1,0,2,3:T(2,128)(2,1)} %copy.44), calls=%async_computation | async-start | bytes 6291456 | tf_op jit(solution)/shard_map/all_to_all | solution.py:78
  20.5 108.5 %reduce-scatter.2.cloned.1.call-start = ((), (), s32[]{:S(2)}) async-start(), calls=%async_computation.3 | async-start | bytes 1146880 | tf_op jit(solution)/shard_map/reduce_scatter | solution.py:94
  85.9 3.7 %copy-start.1 = (f32[2048,768]{0,1:T(8,128)}, f32[2048,768]{0,1:T(8,128)S(1)}, u32[]{:S(2)}) copy-start(f32[2048,768]{0,1:T(8,128)S(1)} %fusion) | copy-start | bytes 18874372
  102.3 1.5 copy-start.3
  130.8 20.0 %all-to-all-start.1 = ((f32[32,8,224]{2,1,0:T(8,128)}), f32[32,8,224]{2,1,0:T(8,128)S(1)}, u32[]{:S(2)}, u32[]{:S(2)}) async-start(f32[32,8,224]{2,1,0:T(8,128)} %bitcast.5), calls=%async_computation.2 | async-start | bytes 524288 | tf_op jit(solution)/shard_map/all_to_all | solution.py:97
  154.4 3.7 %copy-start.2 = (pred[5,32,16,256]{3,2,1,0:T(8,128)(4,1)S(1)}, pred[5,32,16,256]{3,2,1,0:T(8,128)(4,1)}, u32[]{:S(2)}) copy-start(pred[5,32,16,256]{3,2,1,0:T(8,128)(4,1)} %broadcast_and_fusion) | copy-start | bytes 1966084
  158.1 10.0 %copy-start.4 = (s32[3,2]{0,1:T(2,128)S(1)}, s32[3,2]{0,1:T(2,128)}, u32[]{:S(2)}) copy-start(s32[3,2]{0,1:T(2,128)} %param.9) | copy-start | bytes 76
  162.4 19.8 %collective-permute-start = (f32[8,12,256]{2,1,0:T(8,128)S(1)}, f32[8,12,256]{2,1,0:T(8,128)S(1)}, u32[]{:S(2)}, u32[]{:S(2)}) collective-permute-start(f32[8,12,256]{2,1,0:T(8,128)S(1)} %get-tuple-element.12), channel_id=1, source_target_pairs={{128,0},{129,1},{130,2},{131,3},{132,4},{133,5},{134,6},{135,7},{1... | collective-permute-start | bytes 294920 | tf_op jit(solution)/shard_map/ppermute | solution.py:106
Sparse Core Ops, SparseCore 0:
  103.9 25.0 reduce-scatter.1
